TPU v7x, 256 devices: a whole 4x4x8 slice. The times are simulated.
256 devices in a mesh: tm: 64 (over y, z_lo, x, core), floor: 4 (over z_hi).
Axes of the slice: x: 4, y: 4, z: 8 (z_hi: 4, z_lo: 2; z = z_hi * 2 + z_lo), core: 2. Of those that a mesh axis runs over, the one named last changes fastest.
Arguments:
- samples: bfloat16 [64, 16, 32768], P('tm', None, 'floor'), may hold values from -6 to 6
- operator: bfloat16 [64, 512, 32768], P('tm', None, 'floor'), may hold values from -0.00390625 to 0.00390625
Outputs:
- sensor_data: bfloat16 [64, 16, 512], P('tm', None, 'floor')
All inputs are finite; a program needn't handle non-finite values.
Results may differ from a plain program's by a relative error of at most 0.0013.
Values may be sent and summed in bfloat16 or wider, within the bound.
No kernel may reach another device: no remote copies, remote signals or barrier semaphores. Data moves between devices by JAX's collectives and lax.ppermute only.
A program may use at most 64 MiB of HBM per device.

v0:
```python
import jax
import jax.numpy as jnp
from jax import lax
from jax.sharding import PartitionSpec as P


def local(samples, operator):
    lag = lax.axis_index("tm")
    blocks = lax.axis_size("tm")
    kernel = operator[0]
    images = jnp.einsum(
        "cki,si->cks",
        lax.all_gather(samples, "tm", axis=0, tiled=True),
        kernel,
        preferred_element_type=jnp.float32,
    )
    padded = jnp.pad(images, ((blocks, 0), (0, 0), (0, 0)))
    shifted = lax.dynamic_slice_in_dim(padded, blocks - lag, blocks, 0)
    mine = lax.all_to_all(shifted, "tm", 0, 0, tiled=True).sum(0)
    parts = mine.reshape(mine.shape[0], lax.axis_size("floor"), -1).swapaxes(0, 1)
    records = lax.all_to_all(parts, "floor", 0, 0, tiled=True).sum(0)
    return records[None].astype(jnp.bfloat16)


def solution(mesh):
    placed = (P("tm", None, "floor"), P("tm", None, "floor"))
    return jax.shard_map(
        local, mesh=mesh, in_specs=placed, out_specs=P("tm", None, "floor"), check_vma=False
    )
```

profile of v0, /device:TPU:1, one launch (start us, length us, event | category | flops | bytes accessed | tf_op | source)
XLA Modules:
  0.0 216.1 jit_solution(414119215055207284)
XLA Ops:
  6.5 0.0 all-gather.2.cloned.1.call-start
  6.5 0.7 all-gather.2.cloned.1.call-update
  7.3 131.9 %all-gather.2.cloned.1.call-done = bf16[64,16,8192]{2,1,0:T(8,128)(2,1)} async-done(((bf16[1,16,8192]{2,1,0:T(8,128)(2,1)}), bf16[64,16,8192]{2,1,0:T(8,128)(2,1)}) %all-gather.2.cloned.1.call-update) | async-done | bytes 16777232 | tf_op jit(solution)/shard_map/all_gather | solution.py:13
  139.1 21.5 %fusion = f32[128,16,512]{2,1,0:T(8,128)S(1)} fusion(bf16[64,16,8192]{2,1,0:T(8,128)(2,1)} %all-gather.2.cloned.1.call-done, bf16[1,512,8192]{2,1,0:T(8,128)(2,1)} %param.3), kind=kOutput, calls=%fused_computation | convolution fusion | flops 8589934592 | bytes 29360128 | tf_op jit(solution)/shard_map/jit(_pad)/pad | solution.py:17
  160.7 0.2 constant_dynamic-slice_fusion
  160.9 35.0 %all_to_all.10 = f32[64,16,512]{2,1,0:T(8,128)S(1)} all-to-all(f32[64,16,512]{2,1,0:T(8,128)S(1)} %constant_dynamic-slice_fusion), channel_id=1, replica_groups=mesh['tm'=64,'floor'=4] {'tm'}, dimensions={0} | all-to-all | bytes 4194304 | tf_op jit(solution)/shard_map/all_to_all | solution.py:19
  195.9 0.1 reduce_sum.18
  196.1 12.6 %all_to_all.11 = f32[4,16,128]{2,1,0:T(8,128)S(1)} all-to-all(f32[4,16,128]{2,1,0:T(8,128)S(1)} %copy.3), channel_id=1, replica_groups=mesh['tm'=64,'floor'=4] {'floor'}, dimensions={0} | all-to-all | bytes 65536 | tf_op jit(solution)/shard_map/all_to_all | solution.py:21
  208.7 0.6 reduce_sum.19
  (2 shorter events, 0.0 us)
Async XLA Ops:
  6.5 132.6 %all-gather.2.cloned.1.call-start = ((), (), s32[]{:S(2)}) async-start(), calls=%async_computation.2 | async-start | bytes 17039360 | tf_op jit(solution)/shard_map/all_gather | solution.py:13
Sparse Core Ops, SparseCore 0:
  9.2 129.8 all-gather.1
where the time goes:
time: 216 us
  waiting for transfers between devices  133 us (62%)
  blocking collectives  47.6 us (22%)
  matrix products  21.5 us (10%)
  between operations  13.4 us (6%)
    all_gather x1, waiting for transfers between devices, local(): lax.all_gather(samples, 'tm', axis=0, tiled=True)  132 us
    all_to_all x1, blocking collectives, local(): mine = lax.all_to_all(shifted, 'tm', 0, 0, tiled=True).sum(0)  35 us
    pad x1, matrix products, local(): padded = jnp.pad(images, ((blocks, 0), (0, 0), (0, 0)))  21.5 us
    all_to_all x1, blocking collectives, local(): records = lax.all_to_all(parts, 'floor', 0, 0, tiled=True).sum(0)  12.6 us
  transfers between devices with their start and end apart: 1, of which 1 were waited for; matrix products, arithmetic and copies ran while one was open for 0% of the time, Pallas kernels for 0%

commit v1 on v0

--- a/solution.py
+++ b/solution.py
@@ -10,7 +10,9 @@
     kernel = operator[0]
     images = jnp.einsum(
         "cki,si->cks",
-        lax.all_gather(samples, "tm", axis=0, tiled=True),
+        jnp.concatenate(
+            lax.all_to_all(jnp.stack([samples] * lax.axis_size("tm")), "tm", 0, 0), axis=0
+        ),
         kernel,
         preferred_element_type=jnp.float32,
     )

time: 216 us -> 327 us (1.51)
  waiting for transfers between devices: 133 us -> 237 us
  between operations: 13.4 us -> 0.05 us
  starting transfers between devices: 0.01 us -> 10.5 us
  local copies, waits for them, and re-layouts: 0.21 us -> 6.89 us
    all_to_all x0 -> x1, waiting for transfers between devices: none -> 237 us  [local(): lax.all_to_all(jnp.stack([samples] * lax.axis_size('tm')), 'tm', 0, 0)]
    all_gather x1 -> x0, waiting for transfers between devices: 132 us -> none  [local(): lax.all_gather(samples, 'tm', axis=0, tiled=True)]
    all_to_all x0 -> x1, starting transfers between devices: none -> 10.5 us  [local(): lax.all_to_all(jnp.stack([samples] * lax.axis_size('tm')), 'tm', 0, 0)]
    another operation x0 -> x1, local copies, waits for them, and re-layouts: none -> 6.68 us  [local(): jnp.stack([samples] * lax.axis_size('tm'))]
where the time goes in v1:
time: 327 us
  waiting for transfers between devices  237 us (72%)
  blocking collectives  49.7 us (15%)
  matrix products  21.5 us (7%)
  starting transfers between devices  10.5 us (3%)
  local copies, waits for them, and re-layouts  6.89 us (2%)
    all_to_all x1, waiting for transfers between devices, local(): lax.all_to_all(jnp.stack([samples] * lax.axis_size('tm')), 'tm', 0, 0)  237 us
    all_to_all x1, blocking collectives, local(): mine = lax.all_to_all(shifted, 'tm', 0, 0, tiled=True).sum(0)  35.9 us
    pad x1, matrix products, local(): padded = jnp.pad(images, ((blocks, 0), (0, 0), (0, 0)))  21.5 us
    all_to_all x1, blocking collectives, local(): records = lax.all_to_all(parts, 'floor', 0, 0, tiled=True).sum(0)  13.8 us
    all_to_all x1, starting transfers between devices, local(): lax.all_to_all(jnp.stack([samples] * lax.axis_size('tm')), 'tm', 0, 0)  10.5 us
    another operation x1, local copies, waits for them, and re-layouts, local(): jnp.stack([samples] * lax.axis_size('tm'))  6.68 us
  transfers between devices with their start and end apart: 1, of which 1 were waited for; matrix products, arithmetic and copies ran while one was open for 0% of the time, Pallas kernels for 0%

profile of v1, /device:TPU:1, one launch (start us, length us, event | category | flops | bytes accessed | tf_op | source)
XLA Modules:
  0.0 326.6 jit_solution(758732552583135287)
XLA Ops:
  0.0 6.7 %stack.2 = bf16[64,1,16,8192]{3,2,1,0:T(8,128)(2,1)} broadcast(bf16[16,8192]{1,0:T(8,128)(2,1)} %bitcast.12), dimensions={2,3} | broadcast | bytes 17039360 | tf_op jit(solution)/shard_map/stack | solution.py:14
  6.7 10.5 %all-to-all-start = ((bf16[64,1,16,8192]{3,2,1,0:T(8,128)(2,1)}), bf16[64,1,16,8192]{3,2,1,0:T(8,128)(2,1)}, u32[]{:S(2)}, u32[]{:S(2)}) async-start(bf16[64,1,16,8192]{3,2,1,0:T(8,128)(2,1)} %stack.2), calls=%async_computation | async-start | bytes 33554432 | tf_op jit(solution)/shard_map/all_to_all | solution.py:14
  17.2 237.2 %all-to-all-done = bf16[64,1,16,8192]{3,2,1,0:T(8,128)(2,1)} async-done(((bf16[64,1,16,8192]{3,2,1,0:T(8,128)(2,1)}), bf16[64,1,16,8192]{3,2,1,0:T(8,128)(2,1)}, u32[]{:S(2)}, u32[]{:S(2)}) %all-to-all-start) | async-done | bytes 16777248 | tf_op jit(solution)/shard_map/all_to_all | solution.py:14
  254.4 21.5 %fusion = f32[128,16,512]{2,1,0:T(8,128)S(1)} fusion(bf16[64,1,16,8192]{3,2,1,0:T(8,128)(2,1)} %all-to-all-done, bf16[1,512,8192]{2,1,0:T(8,128)(2,1)} %param.3), kind=kOutput, calls=%fused_computation | convolution fusion | flops 8589934592 | bytes 29360128 | tf_op jit(solution)/shard_map/jit(_pad)/pad | solution.py:19
  275.9 0.2 constant_dynamic-slice_fusion
  276.1 35.9 %all_to_all.15 = f32[64,16,512]{2,1,0:T(8,128)S(1)} all-to-all(f32[64,16,512]{2,1,0:T(8,128)S(1)} %constant_dynamic-slice_fusion), channel_id=1, replica_groups=mesh['tm'=64,'floor'=4] {'tm'}, dimensions={0} | all-to-all | bytes 4194304 | tf_op jit(solution)/shard_map/all_to_all | solution.py:21
  312.0 0.1 reduce_sum.18
  312.2 13.8 %all_to_all.16 = f32[4,16,128]{2,1,0:T(8,128)S(1)} all-to-all(f32[4,16,128]{2,1,0:T(8,128)S(1)} %copy.3), channel_id=1, replica_groups=mesh['tm'=64,'floor'=4] {'floor'}, dimensions={0} | all-to-all | bytes 65536 | tf_op jit(solution)/shard_map/all_to_all | solution.py:23
  326.0 0.6 reduce_sum.19
  (2 shorter events, 0.0 us)
Async XLA Ops:
  6.7 247.7 %all-to-all-start = ((bf16[64,1,16,8192]{3,2,1,0:T(8,128)(2,1)}), bf16[64,1,16,8192]{3,2,1,0:T(8,128)(2,1)}, u32[]{:S(2)}, u32[]{:S(2)}) async-start(bf16[64,1,16,8192]{3,2,1,0:T(8,128)(2,1)} %stack.2), calls=%async_computation | async-start | bytes 33554432 | tf_op jit(solution)/shard_map/all_to_all | solution.py:14
